TPU v7x, 128 devices: a whole 4x4x4 slice. The times are simulated.
128 devices in a mesh: row: 32 (over y, z, core), col: 4 (over x).
Axes of the slice: x: 4, y: 4, z: 4, core: 2. Of those that a mesh axis runs over, the one named last changes fastest.
Arguments:
- matrix: float32 [16384, 16, 512], P('row', 'col'), may hold values from -200 to 200, as said below
Outputs:
- factored: float32 [16384, 16, 512], P('row', 'col')
- upper_rows: float32 [2, 512, 16, 512], P(None, 'row', 'col')
Inputs may be any that keep to these rules, and one draw needn't show every extreme that they name: `matrix`: Real-valued entries; every panel has full column rank.
All inputs are finite; a program needn't handle non-finite values.
Results may differ from a plain program's by a relative error of at most 0.0001.
Values sent between devices are 32-bit elements; how exact they have to be, the bound alone decides.
A program may use at most 128 MiB of HBM per device.

v0:
```python
import jax
import jax.numpy as jnp
from jax import lax
from jax.sharding import PartitionSpec as P

PANELS = 2
HIGH = lax.Precision.HIGHEST


def spread(value, axis, root):
    mine = lax.axis_index(axis) == root
    return lax.psum(jnp.where(mine, value, jnp.zeros_like(value)), axis)


def right_solve(lower, block):
    eye = jnp.eye(lower.shape[0], dtype=jnp.float32)
    inverse = lax.linalg.triangular_solve(lower, eye, left_side=True, lower=True)
    return jnp.dot(block, inverse.T, precision=HIGH)


def gram_of(block):
    return jnp.dot(block.T, block, precision=HIGH)


def on_device(matrix):
    work = matrix
    row_dev, blocks, width = matrix.shape
    half = width // 2
    n_row = lax.axis_size("row")
    n_col = lax.axis_size("col")
    my_col = lax.axis_index("col")
    my_row = lax.axis_index("row")
    share = width // n_row
    scale = jnp.sqrt(jnp.float32(row_dev * n_row))
    number = jnp.arange(blocks) * n_col + my_col
    pieces = []
    for k in range(PANELS):
        root = k % n_col
        slot = k // n_col
        owner = my_col == root
        panel = work[:, slot, :]
        first = panel[:, :half]
        second = panel[:, half:]
        lower_one = jnp.linalg.cholesky(lax.psum(gram_of(first), "row"))
        basis_one = right_solve(lower_one, first)
        inner = lax.psum(jnp.dot(basis_one.T, second, precision=HIGH), "row")
        rest = second - jnp.dot(basis_one, inner, precision=HIGH)
        lower_two = jnp.linalg.cholesky(lax.psum(gram_of(rest), "row"))
        basis_two = right_solve(lower_two, rest)
        local_basis = jnp.concatenate([basis_one, basis_two], axis=1)
        top = jnp.concatenate([lower_one.T, inner], axis=1)
        bottom = jnp.concatenate([jnp.zeros((half, half), jnp.float32), lower_two.T], axis=1)
        upper = jnp.concatenate([top, bottom], axis=0)
        basis = spread(local_basis, "col", root)
        keep = (number > k).astype(jnp.float32)
        terms = jnp.einsum("rk,rbc->kbc", basis, work, precision=HIGH) * keep[None, :, None]
        weights = lax.psum(terms, "row")
        mine = lax.dynamic_slice_in_dim(weights, my_row * share, share, 0)
        work = work - jnp.einsum("rk,kbc->rbc", basis, weights, precision=HIGH)
        work = work.at[:, slot, :].set(jnp.where(owner, basis * scale, work[:, slot, :]))
        upper_share = lax.dynamic_slice_in_dim(upper, my_row * share, share, 0)
        mine = mine.at[:, slot, :].set(jnp.where(owner, upper_share, mine[:, slot, :]))
        pieces.append(mine)
    return (work, jnp.stack(pieces, axis=0))


def solution(mesh):
    placed = (P("row", "col", None),)
    return jax.shard_map(
        on_device,
        mesh=mesh,
        in_specs=placed,
        out_specs=(P("row", "col", None), P(None, "row", "col", None)),
        check_vma=False,
    )
```

profile of v0, /device:TPU:1, one launch (start us, length us, event | category | flops | bytes accessed | tf_op | source)
XLA Modules:
  0.0 1277.8 jit_solution(5746735367781790815)
XLA Ops:
  12.0 105.9 %all-reduce.14.cloned.1.call-done = f32[256,256]{0,1:T(8,128)} async-done(((f32[256,256]{0,1:T(8,128)}), f32[256,256]{0,1:T(8,128)}) %all-reduce.14.cloned.1.call-update) | async-done | bytes 262160 | tf_op jit(solution)/shard_map/psum | solution.py:44
  120.0 11.7 cholesky.214
  131.7 9.8 custom-call.17
  142.0 11.7 cholesky.231
  160.3 19.7 %custom-call.18 = f32[2,128,128]{1,2,0:T(8,128)S(1)} custom-call(f32[2,128,128]{2,1,0:T(8,128)S(1)} %get-tuple-element.78), custom_call_target="InvertDiagBlocksLowerTriangular" | custom-call | tf_op jit(solution)/shard_map/triangular_solve/custom-call.0 | solution.py:17
  183.3 102.1 %all-reduce.16.cloned.1.call-done = f32[256,256]{0,1:T(8,128)} async-done(((f32[256,256]{0,1:T(8,128)}), f32[256,256]{0,1:T(8,128)}) %all-reduce.16.cloned.1.call-update) | async-done | bytes 262160 | tf_op jit(solution)/shard_map/psum | solution.py:46
  289.6 101.7 %all-reduce.18.cloned.1.call-done = f32[256,256]{0,1:T(8,128)} async-done(((f32[256,256]{0,1:T(8,128)}), f32[256,256]{0,1:T(8,128)}) %all-reduce.18.cloned.1.call-update) | async-done | bytes 262160 | tf_op jit(solution)/shard_map/psum | solution.py:48
  393.4 11.7 cholesky.248
  405.1 9.8 custom-call.19
  415.6 11.7 cholesky.265
  434.4 19.7 %custom-call.20 = f32[2,128,128]{1,2,0:T(8,128)S(1)} custom-call(f32[2,128,128]{2,1,0:T(8,128)S(1)} %get-tuple-element.79), custom_call_target="InvertDiagBlocksLowerTriangular" | custom-call | tf_op jit(solution)/shard_map/triangular_solve/custom-call.0 | solution.py:17
  456.8 5.2 copy.42
  462.1 38.5 %all-reduce.20.cloned.1.call-done = f32[512,512]{0,1:T(8,128)} async-done(((f32[512,512]{0,1:T(8,128)}), f32[512,512]{0,1:T(8,128)}) %all-reduce.20.cloned.1.call-update) | async-done | bytes 1048592 | tf_op jit(solution)/shard_map/psum | solution.py:12
  500.6 10.2 convolution_multiply_fusion.1
  510.8 114.6 %all-reduce.22.cloned.1.call-done = f32[512,4,512]{0,2,1:T(8,128)} async-done(((f32[512,4,512]{0,2,1:T(8,128)}), f32[512,4,512]{0,2,1:T(8,128)}) %all-reduce.22.cloned.1.call-update) | async-done | bytes 4194320 | tf_op jit(solution)/shard_map/psum | solution.py:57
  625.4 9.2 convolution_subtract_fusion.1
  638.7 101.8 %all-reduce.24.cloned.1.call-done = f32[256,256]{0,1:T(8,128)} async-done(((f32[256,256]{0,1:T(8,128)}), f32[256,256]{0,1:T(8,128)}) %all-reduce.24.cloned.1.call-update) | async-done | bytes 262160 | tf_op jit(solution)/shard_map/psum | solution.py:44
  742.5 11.7 cholesky.282
  754.3 9.8 custom-call.21
  764.6 11.7 cholesky.299
  783.5 19.7 %custom-call.22 = f32[2,128,128]{1,2,0:T(8,128)S(1)} custom-call(f32[2,128,128]{2,1,0:T(8,128)S(1)} %get-tuple-element.80), custom_call_target="InvertDiagBlocksLowerTriangular" | custom-call | tf_op jit(solution)/shard_map/triangular_solve/custom-call.0 | solution.py:17
  806.1 102.1 %all-reduce.26.cloned.1.call-done = f32[256,256]{0,1:T(8,128)} async-done(((f32[256,256]{0,1:T(8,128)}), f32[256,256]{0,1:T(8,128)}) %all-reduce.26.cloned.1.call-update) | async-done | bytes 262160 | tf_op jit(solution)/shard_map/psum | solution.py:46
  911.4 102.1 %all-reduce.28.cloned.1.call-done = f32[256,256]{0,1:T(8,128)} async-done(((f32[256,256]{0,1:T(8,128)}), f32[256,256]{0,1:T(8,128)}) %all-reduce.28.cloned.1.call-update) | async-done | bytes 262160 | tf_op jit(solution)/shard_map/psum | solution.py:48
  1015.5 11.7 cholesky.316
  1027.3 9.8 custom-call.23
  1037.8 11.7 cholesky.333
  1057.0 19.7 %custom-call.24 = f32[2,128,128]{1,2,0:T(8,128)S(1)} custom-call(f32[2,128,128]{2,1,0:T(8,128)S(1)} %get-tuple-element.81), custom_call_target="InvertDiagBlocksLowerTriangular" | custom-call | tf_op jit(solution)/shard_map/triangular_solve/custom-call.0 | solution.py:17
  1080.4 42.7 %all-reduce.30.cloned.1.call-done = f32[512,512]{0,1:T(8,128)} async-done(((f32[512,512]{0,1:T(8,128)}), f32[512,512]{0,1:T(8,128)}) %all-reduce.30.cloned.1.call-update) | async-done | bytes 1048592 | tf_op jit(solution)/shard_map/psum | solution.py:12
  1123.1 10.2 convolution_multiply_fusion
  1137.6 110.4 %all-reduce.32.cloned.1.call-done = f32[512,4,512]{0,2,1:T(8,128)} async-done(((f32[512,4,512]{0,2,1:T(8,128)}), f32[512,4,512]{0,2,1:T(8,128)}) %all-reduce.32.cloned.1.call-update) | async-done | bytes 4194320 | tf_op jit(solution)/shard_map/psum | solution.py:57
  1252.2 10.5 convolution_subtract_fusion
  1265.1 5.4 copy.60
  (161 shorter events, 89.0 us)
Async XLA Ops:
  7.2 110.7 %all-reduce.14.cloned.1.call-start = ((), (), s32[]{:S(2)}) async-start(), calls=%async_computation | async-start | bytes 524288 | tf_op jit(solution)/shard_map/psum | solution.py:44
  11.9 273.5 %all-reduce.16.cloned.1.call-start = ((), (), s32[]{:S(2)}) async-start(), calls=%async_computation.1 | async-start | bytes 524288 | tf_op jit(solution)/shard_map/psum | solution.py:46
  183.3 208.0 %all-reduce.18.cloned.1.call-start = ((), (), s32[]{:S(2)}) async-start(), calls=%async_computation.2 | async-start | bytes 524288 | tf_op jit(solution)/shard_map/psum | solution.py:48
  289.1 211.4 %all-reduce.20.cloned.1.call-start = ((), (), s32[]{:S(2)}) async-start(), calls=%async_computation.3 | async-start | bytes 2097152 | tf_op jit(solution)/shard_map/psum | solution.py:12
  456.8 168.6 %all-reduce.22.cloned.1.call-start = ((), (), s32[]{:S(2)}) async-start(), calls=%async_computation.4 | async-start | bytes 8388608 | tf_op jit(solution)/shard_map/psum | solution.py:57
  510.7 114.7 %copy-start.2 = (f32[512,512]{0,1:T(8,128)S(1)}, f32[512,512]{0,1:T(8,128)}, u32[]{:S(2)}) copy-start(f32[512,512]{0,1:T(8,128)} %all-reduce.20.cloned.1.call-done) | copy-start | bytes 3145732
  510.7 229.7 %all-reduce.24.cloned.1.call-start = ((), (), s32[]{:S(2)}) async-start(), calls=%async_computation.5 | async-start | bytes 524288 | tf_op jit(solution)/shard_map/psum | solution.py:44
  634.6 2.0 copy-start
  638.2 270.0 %all-reduce.26.cloned.1.call-start = ((), (), s32[]{:S(2)}) async-start(), calls=%async_computation.6 | async-start | bytes 524288 | tf_op jit(solution)/shard_map/psum | solution.py:46
  806.1 207.4 %all-reduce.28.cloned.1.call-start = ((), (), s32[]{:S(2)}) async-start(), calls=%async_computation.7 | async-start | bytes 524288 | tf_op jit(solution)/shard_map/psum | solution.py:48
  911.2 212.0 %all-reduce.30.cloned.1.call-start = ((), (), s32[]{:S(2)}) async-start(), calls=%async_computation.8 | async-start | bytes 2097152 | tf_op jit(solution)/shard_map/psum | solution.py:12
  1079.3 168.7 %all-reduce.32.cloned.1.call-start = ((), (), s32[]{:S(2)}) async-start(), calls=%async_computation.9 | async-start | bytes 8388608 | tf_op jit(solution)/shard_map/psum | solution.py:57
  1133.3 0.9 copy-start.3
  1133.3 114.7 %copy-start.4 = (f32[256,256]{0,1:T(8,128)S(1)}, f32[256,256]{0,1:T(8,128)}, u32[]{:S(2)}) copy-start(f32[256,256]{0,1:T(8,128)} %all-reduce.26.cloned.1.call-done) | copy-start | bytes 786436
  1133.3 114.7 %copy-start.5 = (f32[256,256]{0,1:T(8,128)S(1)}, f32[256,256]{0,1:T(8,128)}, u32[]{:S(2)}) copy-start(f32[256,256]{0,1:T(8,128)} %get-tuple-element.132) | copy-start | bytes 786436
  1133.3 114.7 %copy-start.6 = (f32[256,256]{0,1:T(8,128)S(1)}, f32[256,256]{0,1:T(8,128)}, u32[]{:S(2)}) copy-start(f32[256,256]{0,1:T(8,128)} %get-tuple-element.130) | copy-start | bytes 786436
  1135.6 116.6 %copy-start.1 = (f32[512,512]{0,1:T(8,128)S(1)}, f32[512,512]{0,1:T(8,128)}, u32[]{:S(2)}) copy-start(f32[512,512]{0,1:T(8,128)} %all-reduce.30.cloned.1.call-done) | copy-start | bytes 3145732
Sparse Core Ops, SparseCore 0:
  12.0 105.7 all-reduce.13
  183.4 102.0 all-reduce.15
  289.3 101.9 all-reduce.17
  456.9 43.6 all-reduce.19
  510.9 114.5 all-reduce.21
  638.4 102.0 all-reduce.23
  806.2 101.9 all-reduce.25
  911.4 101.9 all-reduce.27
  1079.4 43.6 all-reduce.29
  1133.5 114.5 all-reduce.31
where the time goes:
time: 1290 us; the launch traced here: 1280 us
  waiting for transfers between devices  922 us (71%)
  other arithmetic  229 us (18%)
  matrix products  60.8 us (5%)
  local copies, waits for them, and re-layouts  43 us (3%)
  between operations  20.3 us (2%)
    psum x2, waiting for transfers between devices, on_device(): weights = lax.psum(terms, 'row')  225 us
    psum x2, waiting for transfers between devices, on_device(): lower_one = jnp.linalg.cholesky(lax.psum(gram_of(first), 'row'))  208 us
    psum x2, waiting for transfers between devices, on_device(): inner = lax.psum(jnp.dot(basis_one.T, second, precision=HIGH), 'row')  204 us
    psum x2, waiting for transfers between devices, on_device(): lower_two = jnp.linalg.cholesky(lax.psum(gram_of(rest), 'row'))  204 us
    psum x2, waiting for transfers between devices, spread(): return lax.psum(jnp.where(mine, value, jnp.zeros_like(value)), axis)  81.2 us
    another operation x5, other arithmetic, right_solve(): lax.linalg.triangular_solve(lower, eye, left_side=True, lower=True)  78.7 us
    another operation x14, other arithmetic, on_device(): lower_two = jnp.linalg.cholesky(lax.psum(gram_of(rest), 'row'))  69.3 us
    another operation x13, other arithmetic, on_device(): lower_one = jnp.linalg.cholesky(lax.psum(gram_of(first), 'row'))  68.6 us
  transfers between devices with their start and end apart: 10, of which 10 were waited for; matrix products, arithmetic and copies ran while one was open for 1% of the time, Pallas kernels for 0%

commit v1 on v0

--- a/solution.py
+++ b/solution.py
@@ -43,7 +43,9 @@
         second = panel[:, half:]
         lower_one = jnp.linalg.cholesky(lax.psum(gram_of(first), "row"))
         basis_one = right_solve(lower_one, first)
-        inner = lax.psum(jnp.dot(basis_one.T, second, precision=HIGH), "row")
+        block_2 = jnp.dot(basis_one.T, second, precision=HIGH)
+        parts = lax.all_gather(block_2, "row")
+        inner = jnp.sum(parts, axis=0)
         rest = second - jnp.dot(basis_one, inner, precision=HIGH)
         lower_two = jnp.linalg.cholesky(lax.psum(gram_of(rest), "row"))
         basis_two = right_solve(lower_two, rest)

time: 1290 us -> 1190 us (0.922)
  waiting for transfers between devices: 922 us -> 822 us
    psum x2 -> x0, waiting for transfers between devices: 204 us -> none  [on_device(): inner = lax.psum(jnp.dot(basis_one.T, second, precision=HIGH), 'row')]
    all_gather x0 -> x2, waiting for transfers between devices: none -> 106 us  [on_device(): parts = lax.all_gather(block_2, 'row')]
where the time goes in v1:
time: 1190 us; the launch traced here: 1180 us
  waiting for transfers between devices  822 us (69%)
  other arithmetic  239 us (20%)
  matrix products  58.5 us (5%)
  local copies, waits for them, and re-layouts  42.9 us (4%)
  between operations  20.2 us (2%)
    psum x2, waiting for transfers between devices, on_device(): weights = lax.psum(terms, 'row')  225 us
    psum x2, waiting for transfers between devices, on_device(): lower_one = jnp.linalg.cholesky(lax.psum(gram_of(first), 'row'))  208 us
    psum x2, waiting for transfers between devices, on_device(): lower_two = jnp.linalg.cholesky(lax.psum(gram_of(rest), 'row'))  203 us
    all_gather x2, waiting for transfers between devices, on_device(): parts = lax.all_gather(block_2, 'row')  106 us
    psum x2, waiting for transfers between devices, spread(): return lax.psum(jnp.where(mine, value, jnp.zeros_like(value)), axis)  81.2 us
    another operation x5, other arithmetic, right_solve(): lax.linalg.triangular_solve(lower, eye, left_side=True, lower=True)  78.7 us
    another operation x14, other arithmetic, on_device(): lower_two = jnp.linalg.cholesky(lax.psum(gram_of(rest), 'row'))  69.2 us
    another operation x13, other arithmetic, on_device(): lower_one = jnp.linalg.cholesky(lax.psum(gram_of(first), 'row'))  68.6 us
  transfers between devices with their start and end apart: 10, of which 10 were waited for; matrix products, arithmetic and copies ran while one was open for 1% of the time, Pallas kernels for 0%

profile of v1, /device:TPU:1, one launch (start us, length us, event | category | flops | bytes accessed | tf_op | source)
XLA Modules:
  0.0 1185.0 jit_solution(15816258758011770218)
XLA Ops:
  12.0 105.9 %all-reduce.12.cloned.1.call-done = f32[256,256]{0,1:T(8,128)} async-done(((f32[256,256]{0,1:T(8,128)}), f32[256,256]{0,1:T(8,128)}) %all-reduce.12.cloned.1.call-update) | async-done | bytes 262160 | tf_op jit(solution)/shard_map/psum | solution.py:44
  120.0 11.7 cholesky.214
  131.7 9.8 custom-call.17
  142.0 11.7 cholesky.231
  161.0 19.7 %custom-call.18 = f32[2,128,128]{1,2,0:T(8,128)S(1)} custom-call(f32[2,128,128]{2,1,0:T(8,128)S(1)} %get-tuple-element.78), custom_call_target="InvertDiagBlocksLowerTriangular" | custom-call | tf_op jit(solution)/shard_map/triangular_solve/custom-call.0 | solution.py:17
  183.6 52.8 %all-gather.5.cloned.1.call-done = f32[8192,256]{1,0:T(8,128)} async-done(((f32[256,256]{1,0:T(8,128)}), f32[8192,256]{1,0:T(8,128)}) %all-gather.5.cloned.1.call-update) | async-done | bytes 8388624 | tf_op jit(solution)/shard_map/all_gather | solution.py:47
  243.5 101.4 %all-reduce.14.cloned.1.call-done = f32[256,256]{0,1:T(8,128)} async-done(((f32[256,256]{0,1:T(8,128)}), f32[256,256]{0,1:T(8,128)}) %all-reduce.14.cloned.1.call-update) | async-done | bytes 262160 | tf_op jit(solution)/shard_map/psum | solution.py:50
  347.0 11.7 cholesky.248
  358.7 9.8 custom-call.19
  369.2 11.7 cholesky.265
  388.7 19.7 %custom-call.20 = f32[2,128,128]{1,2,0:T(8,128)S(1)} custom-call(f32[2,128,128]{2,1,0:T(8,128)S(1)} %get-tuple-element.79), custom_call_target="InvertDiagBlocksLowerTriangular" | custom-call | tf_op jit(solution)/shard_map/triangular_solve/custom-call.0 | solution.py:17
  411.1 5.2 copy.68
  416.4 38.5 %all-reduce.16.cloned.1.call-done = f32[512,512]{0,1:T(8,128)} async-done(((f32[512,512]{0,1:T(8,128)}), f32[512,512]{0,1:T(8,128)}) %all-reduce.16.cloned.1.call-update) | async-done | bytes 1048592 | tf_op jit(solution)/shard_map/psum | solution.py:12
  454.9 10.2 convolution_multiply_fusion.1
  465.1 114.5 %all-reduce.18.cloned.1.call-done = f32[512,4,512]{0,2,1:T(8,128)} async-done(((f32[512,4,512]{0,2,1:T(8,128)}), f32[512,4,512]{0,2,1:T(8,128)}) %all-reduce.18.cloned.1.call-update) | async-done | bytes 4194320 | tf_op jit(solution)/shard_map/psum | solution.py:59
  579.7 9.2 convolution_subtract_fusion.1
  592.9 101.8 %all-reduce.20.cloned.1.call-done = f32[256,256]{0,1:T(8,128)} async-done(((f32[256,256]{0,1:T(8,128)}), f32[256,256]{0,1:T(8,128)}) %all-reduce.20.cloned.1.call-update) | async-done | bytes 262160 | tf_op jit(solution)/shard_map/psum | solution.py:44
  696.8 11.7 cholesky.282
  708.5 9.8 custom-call.21
  718.8 11.7 cholesky.299
  737.6 19.7 %custom-call.22 = f32[2,128,128]{1,2,0:T(8,128)S(1)} custom-call(f32[2,128,128]{2,1,0:T(8,128)S(1)} %get-tuple-element.80), custom_call_target="InvertDiagBlocksLowerTriangular" | custom-call | tf_op jit(solution)/shard_map/triangular_solve/custom-call.0 | solution.py:17
  760.2 52.8 %all-gather.7.cloned.1.call-done = f32[8192,256]{1,0:T(8,128)} async-done(((f32[256,256]{1,0:T(8,128)}), f32[8192,256]{1,0:T(8,128)}) %all-gather.7.cloned.1.call-update) | async-done | bytes 8388624 | tf_op jit(solution)/shard_map/all_gather | solution.py:47
  819.3 101.6 %all-reduce.22.cloned.1.call-done = f32[256,256]{0,1:T(8,128)} async-done(((f32[256,256]{0,1:T(8,128)}), f32[256,256]{0,1:T(8,128)}) %all-reduce.22.cloned.1.call-update) | async-done | bytes 262160 | tf_op jit(solution)/shard_map/psum | solution.py:50
  922.9 11.7 cholesky.316
  934.7 9.8 custom-call.23
  945.2 11.7 cholesky.333
  964.2 19.7 %custom-call.24 = f32[2,128,128]{1,2,0:T(8,128)S(1)} custom-call(f32[2,128,128]{2,1,0:T(8,128)S(1)} %get-tuple-element.81), custom_call_target="InvertDiagBlocksLowerTriangular" | custom-call | tf_op jit(solution)/shard_map/triangular_solve/custom-call.0 | solution.py:17
  987.7 42.7 %all-reduce.24.cloned.1.call-done = f32[512,512]{0,1:T(8,128)} async-done(((f32[512,512]{0,1:T(8,128)}), f32[512,512]{0,1:T(8,128)}) %all-reduce.24.cloned.1.call-update) | async-done | bytes 1048592 | tf_op jit(solution)/shard_map/psum | solution.py:12
  1030.4 10.2 convolution_multiply_fusion
  1045.0 110.3 %all-reduce.26.cloned.1.call-done = f32[512,4,512]{0,2,1:T(8,128)} async-done(((f32[512,4,512]{0,2,1:T(8,128)}), f32[512,4,512]{0,2,1:T(8,128)}) %all-reduce.26.cloned.1.call-update) | async-done | bytes 4194320 | tf_op jit(solution)/shard_map/psum | solution.py:59
  1159.4 10.5 convolution_subtract_fusion
  1172.3 5.4 copy.87
  (165 shorter events, 95.7 us)
Async XLA Ops:
  7.2 110.7 %all-reduce.12.cloned.1.call-start = ((), (), s32[]{:S(2)}) async-start(), calls=%async_computation | async-start | bytes 524288 | tf_op jit(solution)/shard_map/psum | solution.py:44
  11.9 224.5 %all-gather.5.cloned.1.call-start = ((), (), s32[]{:S(2)}) async-start(), calls=%async_computation.8 | async-start | bytes 8650752 | tf_op jit(solution)/shard_map/all_gather | solution.py:47
  183.5 161.4 %all-reduce.14.cloned.1.call-start = ((), (), s32[]{:S(2)}) async-start(), calls=%async_computation.1 | async-start | bytes 524288 | tf_op jit(solution)/shard_map/psum | solution.py:50
  243.1 211.8 %all-reduce.16.cloned.1.call-start = ((), (), s32[]{:S(2)}) async-start(), calls=%async_computation.2 | async-start | bytes 2097152 | tf_op jit(solution)/shard_map/psum | solution.py:12
  411.1 168.6 %all-reduce.18.cloned.1.call-start = ((), (), s32[]{:S(2)}) async-start(), calls=%async_computation.3 | async-start | bytes 8388608 | tf_op jit(solution)/shard_map/psum | solution.py:59
  465.0 114.6 %copy-start.2 = (f32[512,512]{0,1:T(8,128)S(1)}, f32[512,512]{0,1:T(8,128)}, u32[]{:S(2)}) copy-start(f32[512,512]{0,1:T(8,128)} %all-reduce.16.cloned.1.call-done) | copy-start | bytes 3145732
  465.1 229.6 %all-reduce.20.cloned.1.call-start = ((), (), s32[]{:S(2)}) async-start(), calls=%async_computation.4 | async-start | bytes 524288 | tf_op jit(solution)/shard_map/psum | solution.py:44
  588.9 2.0 copy-start
  592.5 220.6 %all-gather.7.cloned.1.call-start = ((), (), s32[]{:S(2)}) async-start(), calls=%async_computation.9 | async-start | bytes 8650752 | tf_op jit(solution)/shard_map/all_gather | solution.py:47
  760.2 160.7 %all-reduce.22.cloned.1.call-start = ((), (), s32[]{:S(2)}) async-start(), calls=%async_computation.5 | async-start | bytes 524288 | tf_op jit(solution)/shard_map/psum | solution.py:50
  819.0 211.3 %all-reduce.24.cloned.1.call-start = ((), (), s32[]{:S(2)}) async-start(), calls=%async_computation.6 | async-start | bytes 2097152 | tf_op jit(solution)/shard_map/psum | solution.py:12
  986.5 168.7 %all-reduce.26.cloned.1.call-start = ((), (), s32[]{:S(2)}) async-start(), calls=%async_computation.7 | async-start | bytes 8388608 | tf_op jit(solution)/shard_map/psum | solution.py:59
  1040.5 0.9 copy-start.3
  1040.5 1.0 copy-start.4
  1040.5 114.7 %copy-start.5 = (f32[256,256]{0,1:T(8,128)S(1)}, f32[256,256]{0,1:T(8,128)}, u32[]{:S(2)}) copy-start(f32[256,256]{0,1:T(8,128)} %get-tuple-element.134) | copy-start | bytes 786436
  1040.5 114.7 %copy-start.6 = (f32[256,256]{0,1:T(8,128)S(1)}, f32[256,256]{0,1:T(8,128)}, u32[]{:S(2)}) copy-start(f32[256,256]{0,1:T(8,128)} %get-tuple-element.132) | copy-start | bytes 786436
  1044.5 114.9 %copy-start.1 = (f32[512,512]{0,1:T(8,128)S(1)}, f32[512,512]{0,1:T(8,128)}, u32[]{:S(2)}) copy-start(f32[512,512]{0,1:T(8,128)} %all-reduce.24.cloned.1.call-done) | copy-start | bytes 3145732
Sparse Core Ops, SparseCore 0:
  12.0 105.7 all-reduce.11
  183.6 52.7 all-gather.4
  243.2 101.6 all-reduce.13
  411.2 43.6 all-reduce.15
  465.2 114.4 all-reduce.17
  592.6 102.0 all-reduce.19
  760.3 52.7 all-gather.6
  819.2 101.6 all-reduce.21
  986.7 43.6 all-reduce.23
  1040.7 114.5 all-reduce.25
